TPU v7x, 32 devices: a whole 2x2x4 slice. The times are simulated.
32 devices in a mesh: rep: 4 (over y, x), shard: 8 (over z, core).
Axes of the slice: x: 2, y: 2, z: 4, core: 2. Of those that a mesh axis runs over, the one named last changes fastest.
Arguments:
- hidden_in: float32 [4096, 768], P(('rep', 'shard')), may hold values from -6 to 6
- doc_ids: int32 [32, 128], P(('rep', 'shard')), may hold values from 0 to 3, never falling along the last dimension, each value on 1 to 64 neighbouring positions
- cotangent: float32 [4096, 768], P(('rep', 'shard')), may hold values from -6 to 6
- pre_gain: float32 [1, 768], P(None, 'shard'), may hold values from 0.25 to 1.75
- pre_shift: float32 [1, 768], P(None, 'shard'), may hold values from -3 to 3
- qkv_weight: float32 [1, 768, 2304], P(None, 'shard'), may hold values from -0.21875 to 0.21875
- query_bias: float32 [1, 768], P(None, 'shard'), may hold values from -3 to 3
- value_bias: float32 [1, 768], P(None, 'shard'), may hold values from -3 to 3
- out_weight: float32 [1, 768, 768], P(None, 'shard'), may hold values from -0.875 to 0.875
- out_bias: float32 [1, 768], P(None, 'shard'), may hold values from -3 to 3
- post_gain: float32 [1, 768], P(None, 'shard'), may hold values from 0.25 to 1.75
- post_shift: float32 [1, 768], P(None, 'shard'), may hold values from -3 to 3
- up_weight: float32 [1, 768, 3072], P(None, 'shard'), may hold values from -0.21875 to 0.21875
- up_bias: float32 [1, 3072], P(None, 'shard'), may hold values from -3 to 3
- down_weight: float32 [1, 3072, 768], P(None, 'shard'), may hold values from -0.109375 to 0.109375
- down_bias: float32 [1, 768], P(None, 'shard'), may hold values from -3 to 3
Outputs:
- hidden_out: float32 [4096, 768], P(('rep', 'shard'))
- input_grad: float32 [4096, 768], P(('rep', 'shard'))
- grad_pre_gain: float32 [1, 768], P(None, 'shard')
- grad_pre_shift: float32 [1, 768], P(None, 'shard')
- grad_qkv_weight: float32 [1, 768, 2304], P(None, 'shard')
- grad_query_bias: float32 [1, 768], P(None, 'shard')
- grad_value_bias: float32 [1, 768], P(None, 'shard')
- grad_out_weight: float32 [1, 768, 768], P(None, 'shard')
- grad_out_bias: float32 [1, 768], P(None, 'shard')
- grad_post_gain: float32 [1, 768], P(None, 'shard')
- grad_post_shift: float32 [1, 768], P(None, 'shard')
- grad_up_weight: float32 [1, 768, 3072], P(None, 'shard')
- grad_up_bias: float32 [1, 3072], P(None, 'shard')
- grad_down_weight: float32 [1, 3072, 768], P(None, 'shard')
- grad_down_bias: float32 [1, 768], P(None, 'shard')
Inputs may be any that keep to these rules, and one draw needn't show every extreme that they name: `doc_ids`: along each row the document number never falls; all 4 documents appear in every row, each of 1 to 64 tokens, one of exactly 64.
All inputs are finite; a program needn't handle non-finite values.
Results may differ from a plain program's by a relative error of at most 0.018.
Values may be sent and summed in bfloat16 or wider, within the bound.
No kernel may reach another device: no remote copies, remote signals or barrier semaphores. Data moves between devices by JAX's collectives and lax.ppermute only.
A program may use at most 128 MiB of HBM per device.

v0:
```python
import jax
import jax.numpy as jnp
from jax import lax
from jax.sharding import PartitionSpec as P

HEADS = 12
HEAD = 64
LAYERS = 1
EPS = 1e-05
GELU_C = 0.7978845608028654
NEG_FILL = -1e30


def norm(values_in, gains, shifts):
    average = jnp.mean(values_in, axis=-1, keepdims=True)
    centred = values_in - average
    spread = jnp.mean(centred * centred, axis=-1, keepdims=True)
    return centred * lax.rsqrt(spread + EPS) * gains + shifts


def gelu_tanh(values_in):
    return (
        0.5
        * values_in
        * (1.0 + jnp.tanh(GELU_C * (values_in + 0.044715 * values_in * values_in * values_in)))
    )


def project(left, right):
    return jnp.dot(left, right, preferred_element_type=jnp.float32)


def project_back(left, right):
    return lax.dot_general(
        left, right, (((0,), (0,)), ((), ())), preferred_element_type=jnp.float32
    )


def project_trans(left, right):
    return lax.dot_general(
        left, right, (((1,), (1,)), ((), ())), preferred_element_type=jnp.float32
    )


def layer_slices(shards, layer_index):
    return tuple((stacked[layer_index].astype(jnp.bfloat16) for stacked in shards))


def fetch_forward(shards, layer_index):
    parts = layer_slices(shards, layer_index)
    return (
        lax.all_gather(parts[0], "shard", axis=0, tiled=True),
        lax.all_gather(parts[1], "shard", axis=0, tiled=True),
        lax.all_gather(parts[2], "shard", axis=0, tiled=True),
        lax.all_gather(parts[3], "shard", axis=0, tiled=True),
        lax.all_gather(parts[4], "shard", axis=0, tiled=True),
        lax.all_gather(parts[5], "shard", axis=0, tiled=True),
        lax.all_gather(parts[6], "shard", axis=0, tiled=True),
        lax.all_gather(parts[7], "shard", axis=0, tiled=True),
        lax.all_gather(parts[8], "shard", axis=0, tiled=True),
        lax.all_gather(parts[9], "shard", axis=0, tiled=True),
        lax.all_gather(parts[10], "shard", axis=0, tiled=True),
        lax.all_gather(parts[11], "shard", axis=0, tiled=True),
        lax.all_gather(parts[12], "shard", axis=0, tiled=True),
    )


def reduce_nested_rest(grads):
    owned = (
        lax.psum_scatter(
            grads[0].astype(jnp.bfloat16), "shard", scatter_dimension=0, tiled=True
        ).astype(jnp.float32),
        lax.psum_scatter(
            grads[1].astype(jnp.bfloat16), "shard", scatter_dimension=0, tiled=True
        ).astype(jnp.float32),
        lax.psum_scatter(
            grads[2].astype(jnp.bfloat16), "shard", scatter_dimension=0, tiled=True
        ).astype(jnp.float32),
        lax.psum_scatter(
            grads[3].astype(jnp.bfloat16), "shard", scatter_dimension=0, tiled=True
        ).astype(jnp.float32),
        lax.psum_scatter(
            grads[4].astype(jnp.bfloat16), "shard", scatter_dimension=0, tiled=True
        ).astype(jnp.float32),
        lax.psum_scatter(
            grads[5].astype(jnp.bfloat16), "shard", scatter_dimension=0, tiled=True
        ).astype(jnp.float32),
        lax.psum_scatter(
            grads[6].astype(jnp.bfloat16), "shard", scatter_dimension=0, tiled=True
        ).astype(jnp.float32),
        lax.psum_scatter(
            grads[7].astype(jnp.bfloat16), "shard", scatter_dimension=0, tiled=True
        ).astype(jnp.float32),
        lax.psum_scatter(
            grads[8].astype(jnp.bfloat16), "shard", scatter_dimension=0, tiled=True
        ).astype(jnp.float32),
        lax.psum_scatter(
            grads[9].astype(jnp.bfloat16), "shard", scatter_dimension=0, tiled=True
        ).astype(jnp.float32),
        lax.psum_scatter(
            grads[10].astype(jnp.bfloat16), "shard", scatter_dimension=0, tiled=True
        ).astype(jnp.float32),
    )
    return (
        lax.psum(owned[0].astype(jnp.bfloat16), "rep").astype(jnp.float32),
        lax.psum(owned[1].astype(jnp.bfloat16), "rep").astype(jnp.float32),
        lax.psum(owned[2].astype(jnp.bfloat16), "rep").astype(jnp.float32),
        lax.psum(owned[3].astype(jnp.bfloat16), "rep").astype(jnp.float32),
        lax.psum(owned[4].astype(jnp.bfloat16), "rep").astype(jnp.float32),
        lax.psum(owned[5].astype(jnp.bfloat16), "rep").astype(jnp.float32),
        lax.psum(owned[6].astype(jnp.bfloat16), "rep").astype(jnp.float32),
        lax.psum(owned[7].astype(jnp.bfloat16), "rep").astype(jnp.float32),
        lax.psum(owned[8].astype(jnp.bfloat16), "rep").astype(jnp.float32),
        lax.psum(owned[9].astype(jnp.bfloat16), "rep").astype(jnp.float32),
        lax.psum(owned[10].astype(jnp.bfloat16), "rep").astype(jnp.float32),
    )


def block_scores(query_block, key_rows, doc_block, doc_row, offset):
    query_places = offset + lax.iota(jnp.int32, query_block.shape[0])
    key_places = lax.iota(jnp.int32, key_rows.shape[0])
    allowed = (query_places[:, None] >= key_places[None, :]) & (
        doc_block[:, None] == doc_row[None, :]
    )
    scores = (
        jnp.einsum("qhe,khe->hqk", query_block, key_rows, preferred_element_type=jnp.float32)
        * 0.125
    )
    return jnp.where(allowed[None], scores, NEG_FILL)


def attention_forward(queries, key_rows, value_rows, doc_row):
    length = queries.shape[0]
    rows_block = min(length, 512)
    blocks = length // rows_block

    def one_block(block_index):
        offset = block_index * rows_block
        scores = block_scores(queries, key_rows, doc_row, doc_row, offset)
        highest = jnp.max(scores, axis=-1, keepdims=True)
        log_total = highest + jnp.log(jnp.sum(jnp.exp(scores - highest), axis=-1, keepdims=True))
        weights = jnp.exp(scores - log_total).astype(jnp.bfloat16)
        mixed = jnp.einsum("hqk,khe->qhe", weights, value_rows, preferred_element_type=jnp.float32)
        return (mixed.astype(jnp.bfloat16), log_total)

    mixed, log_totals = lax.map(one_block, jnp.arange(blocks, dtype=jnp.int32))
    return (mixed.reshape(length, -1), log_totals)


def attention_backward(queries, key_rows, value_rows, doc_row, log_totals, grad_mixed):
    length = queries.shape[0]
    rows_block = min(length, 512)
    blocks = length // rows_block

    def one_block(carry, block_index):
        grad_keys, grad_values = carry
        offset = block_index * rows_block
        scores = block_scores(queries, key_rows, doc_row, doc_row, offset)
        weights = jnp.exp(scores - log_totals[block_index])
        grad_values = grad_values + jnp.einsum(
            "hqk,qhe->khe",
            weights.astype(jnp.bfloat16),
            grad_mixed,
            preferred_element_type=jnp.float32,
        )
        grad_weights = jnp.einsum(
            "qhe,khe->hqk", grad_mixed, value_rows, preferred_element_type=jnp.float32
        )
        grad_scores = weights * (
            grad_weights - jnp.sum(grad_weights * weights, axis=-1, keepdims=True)
        )
        grad_scores = grad_scores.astype(jnp.bfloat16)
        grad_query = (
            jnp.einsum("hqk,khe->qhe", grad_scores, key_rows, preferred_element_type=jnp.float32)
            * 0.125
        )
        grad_keys = (
            grad_keys
            + jnp.einsum("hqk,qhe->khe", grad_scores, queries, preferred_element_type=jnp.float32)
            * 0.125
        )
        return ((grad_keys, grad_values), grad_query)

    zeros_kv = jnp.zeros(key_rows.shape, jnp.float32)
    (grad_keys, grad_values), grad_queries = lax.scan(
        one_block, (zeros_kv, zeros_kv), jnp.arange(blocks, dtype=jnp.int32)
    )
    return (
        grad_queries.reshape(length, -1),
        grad_keys.reshape(length, -1),
        grad_values.reshape(length, -1),
    )


def layer_forward(hidden, weights, doc_row):
    (
        pre_gain,
        pre_shift,
        qkv_weight,
        query_bias,
        value_bias,
        out_weight,
        out_bias,
        post_gain,
        post_shift,
        up_weight,
        up_bias,
        down_weight,
        down_bias,
    ) = weights
    rows_here = hidden.shape[0]
    normed = norm(hidden, pre_gain.astype(jnp.float32), pre_shift.astype(jnp.float32)).astype(
        jnp.bfloat16
    )
    bias_row = jnp.concatenate([query_bias, jnp.zeros_like(query_bias), value_bias]).astype(
        jnp.float32
    )
    packed = (project(normed, qkv_weight) + bias_row).astype(jnp.bfloat16)
    shaped = packed.reshape(rows_here, 3, HEADS, HEAD)
    mixed, log_totals = attention_forward(shaped[:, 0], shaped[:, 1], shaped[:, 2], doc_row)
    middle = hidden + project(mixed, out_weight) + out_bias.astype(jnp.float32)
    normed_two = norm(middle, post_gain.astype(jnp.float32), post_shift.astype(jnp.float32)).astype(
        jnp.bfloat16
    )
    pre_act = project(normed_two, up_weight) + up_bias.astype(jnp.float32)
    activ = gelu_tanh(pre_act).astype(jnp.bfloat16)
    output = middle + project(activ, down_weight) + down_bias.astype(jnp.float32)
    stored = (hidden, normed, packed, mixed, log_totals, middle, normed_two, pre_act, activ)
    return (output, stored)


def layer_backward(grad_out, weights, stored, doc_row):
    (
        pre_gain,
        pre_shift,
        qkv_weight,
        query_bias,
        value_bias,
        out_weight,
        out_bias,
        post_gain,
        post_shift,
        up_weight,
        up_bias,
        down_weight,
        down_bias,
    ) = weights
    hidden, normed, packed, mixed, log_totals, middle, normed_two, pre_act, activ = stored
    rows_here, width = hidden.shape
    grad_down = grad_out.astype(jnp.bfloat16)
    activ_columns = lax.all_to_all(activ, "shard", split_axis=1, concat_axis=0, tiled=True)
    group_grads = lax.all_gather(grad_down, "shard", axis=0, tiled=True)
    grad_down_weight = project_back(activ_columns, group_grads)
    width_part = width // lax.axis_size("shard")
    column_total = jnp.sum(group_grads.astype(jnp.float32), axis=0)
    grad_down_bias = lax.dynamic_slice_in_dim(
        column_total, lax.axis_index("shard") * width_part, width_part, 0
    )
    grad_activ = project_trans(grad_down, down_weight)
    unused_gelu, gelu_pull = jax.vjp(gelu_tanh, pre_act)
    grad_pre = gelu_pull(grad_activ)[0].astype(jnp.bfloat16)
    grad_up_weight = project_back(normed_two, grad_pre)
    grad_up_bias = jnp.sum(grad_pre.astype(jnp.float32), axis=0)
    grad_normed_two = project_trans(grad_pre, up_weight)
    unused_post, post_pull = jax.vjp(
        norm, middle, post_gain.astype(jnp.float32), post_shift.astype(jnp.float32)
    )
    grad_middle, grad_post_gain, grad_post_shift = post_pull(grad_normed_two)
    grad_middle = grad_middle + grad_out
    grad_attn = grad_middle.astype(jnp.bfloat16)
    grad_out_weight = project_back(mixed, grad_attn)
    grad_out_bias = jnp.sum(grad_attn.astype(jnp.float32), axis=0)
    grad_mixed = (
        project_trans(grad_attn, out_weight).astype(jnp.bfloat16).reshape(rows_here, HEADS, HEAD)
    )
    shaped = packed.reshape(rows_here, 3, HEADS, HEAD)
    grad_queries, grad_keys, grad_values = attention_backward(
        shaped[:, 0], shaped[:, 1], shaped[:, 2], doc_row, log_totals, grad_mixed
    )
    grad_packed = jnp.concatenate([grad_queries, grad_keys, grad_values], axis=1).astype(
        jnp.bfloat16
    )
    grad_qkv_weight = project_back(normed, grad_packed)
    column_sums = jnp.sum(grad_packed.astype(jnp.float32), axis=0)
    grad_query_bias = column_sums[:width]
    grad_value_bias = column_sums[2 * width :]
    grad_normed = project_trans(grad_packed, qkv_weight)
    unused_pre, pre_pull = jax.vjp(
        norm, hidden, pre_gain.astype(jnp.float32), pre_shift.astype(jnp.float32)
    )
    grad_hidden, grad_pre_gain, grad_pre_shift = pre_pull(grad_normed)
    grads = (
        grad_pre_gain,
        grad_pre_shift,
        grad_qkv_weight,
        grad_query_bias,
        grad_value_bias,
        grad_out_weight,
        grad_out_bias,
        grad_post_gain,
        grad_post_shift,
        grad_up_weight,
        grad_up_bias,
        grad_down_weight,
        grad_down_bias,
    )
    return (grad_hidden + grad_middle, grads)


def on_device(
    hidden_in,
    doc_ids,
    cotangent,
    pre_gain,
    pre_shift,
    qkv_weight,
    query_bias,
    value_bias,
    out_weight,
    out_bias,
    post_gain,
    post_shift,
    up_weight,
    up_bias,
    down_weight,
    down_bias,
):
    shards = (
        pre_gain,
        pre_shift,
        qkv_weight,
        query_bias,
        value_bias,
        out_weight,
        out_bias,
        post_gain,
        post_shift,
        up_weight,
        up_bias,
        down_weight,
        down_bias,
    )
    doc_row = doc_ids[0]
    hidden = hidden_in
    layer_index = 0
    weights = fetch_forward(shards, layer_index)
    hidden, stored = layer_forward(hidden, weights, doc_row)
    gathered_all = [weights]
    stored_all = [stored]
    grad_flow = cotangent
    reduced_all = [None] * LAYERS
    for layer_index in reversed(range(LAYERS)):
        weights = gathered_all[layer_index]
        grad_flow, layer_grads = layer_backward(
            grad_flow, weights, stored_all[layer_index], doc_row
        )
        rest_grads = tuple((layer_grads[member] for member in range(11)))
        rest_sums = reduce_nested_rest(rest_grads)
        down_pair = (layer_grads[11], layer_grads[12])
        down_sums = (
            lax.psum(down_pair[0].astype(jnp.bfloat16), "rep").astype(jnp.float32),
            lax.psum(down_pair[1].astype(jnp.bfloat16), "rep").astype(jnp.float32),
        )
        reduced_all[layer_index] = tuple(rest_sums) + tuple(down_sums)
    stacked = tuple((jnp.stack([reduced_all[0][member]]) for member in range(13)))
    return (
        hidden,
        grad_flow,
        stacked[0],
        stacked[1],
        stacked[2],
        stacked[3],
        stacked[4],
        stacked[5],
        stacked[6],
        stacked[7],
        stacked[8],
        stacked[9],
        stacked[10],
        stacked[11],
        stacked[12],
    )


def solution(mesh):
    in_specs = (
        P(("rep", "shard"), None),
        P(("rep", "shard"), None),
        P(("rep", "shard"), None),
        P(None, "shard"),
        P(None, "shard"),
        P(None, "shard", None),
        P(None, "shard"),
        P(None, "shard"),
        P(None, "shard", None),
        P(None, "shard"),
        P(None, "shard"),
        P(None, "shard"),
        P(None, "shard", None),
        P(None, "shard"),
        P(None, "shard", None),
        P(None, "shard"),
    )
    out_specs = (
        P(("rep", "shard"), None),
        P(("rep", "shard"), None),
        P(None, "shard"),
        P(None, "shard"),
        P(None, "shard", None),
        P(None, "shard"),
        P(None, "shard"),
        P(None, "shard", None),
        P(None, "shard"),
        P(None, "shard"),
        P(None, "shard"),
        P(None, "shard", None),
        P(None, "shard"),
        P(None, "shard", None),
        P(None, "shard"),
    )
    return jax.shard_map(
        on_device, mesh=mesh, in_specs=in_specs, out_specs=out_specs, check_vma=False
    )
```

profile of v0, /device:TPU:0, one launch (start us, length us, event | category | flops | bytes accessed | tf_op | source)
XLA Modules:
  0.0 431.4 jit_solution(6924387649990992)
XLA Ops:
  7.2 2.1 convert_element_type.231
  9.4 0.7 convert_element_type.242
  10.2 0.9 convert_element_type.254
  11.3 0.9 convert_element_type.260
  12.2 0.7 convert_element_type.265
  13.2 0.6 fusion.54
  14.4 0.2 dynamic-update-slice.3
  15.9 32.5 %all-reduce.17 = (bf16[768]{0:T(1024)(128)(2,1)S(1)}, bf16[768]{0:T(1024)(128)(2,1)S(1)}, bf16[768]{0:T(1024)(128)(2,1)S(1)}, bf16[768]{0:T(1024)(128)(2,1)S(1)}...) all-reduce(bf16[768]{0:T(1024)(128)(2,1)S(1)} %dynamic-update-slice, ...), channel_id=6, replica_groups=mesh['rep'=4,'shard'=8] {'shard'}, use_global_device_ids=true, to_apply=%add.3 | all-reduce | flops 5376 | bytes 21504 | tf_op jit(solution)/shard_map/all_gather | solution.py:56
  48.9 12.8 %all-gather.10 = bf16[1,3072]{1,0:T(2,128)(2,1)S(1)} all-gather(bf16[1,384]{1,0:T(2,128)(2,1)S(1)} %convert_element_type.256), channel_id=12, replica_groups=mesh['rep'=4,'shard'=8] {'shard'}, dimensions={1}, use_global_device_ids=true | all-gather | bytes 6912 | tf_op jit(solution)/shard_map/all_gather | solution.py:62
  61.8 2.8 fusion.11
  64.6 0.3 copy.47
  64.9 0.3 fusion.55
  65.4 0.2 convolution_convert_fusion.5
  65.7 13.2 %all-gather.23.cloned.1.call-done = bf16[1,768,768]{2,1,0:T(8,128)(2,1)} async-done(((bf16[1,96,768]{2,1,0:T(8,128)(2,1)}), bf16[1,768,768]{2,1,0:T(8,128)(2,1)}) %all-gather.23.cloned.1.call-update) | async-done | bytes 1179664 | tf_op jit(solution)/shard_map/all_gather | solution.py:57
  78.9 1.7 fusion.56
  80.8 51.2 %all-gather.25.cloned.1.call-done = bf16[1,768,3072]{2,1,0:T(8,128)(2,1)} async-done(((bf16[1,96,3072]{2,1,0:T(8,128)(2,1)}), bf16[1,768,3072]{2,1,0:T(8,128)(2,1)}) %all-gather.25.cloned.1.call-update) | async-done | bytes 4718608 | tf_op jit(solution)/shard_map/all_gather | solution.py:61
  132.0 5.1 %multiply_convert_fusion = (bf16[128,3072]{1,0:T(8,128)(2,1)}, f32[128,3072]{1,0:T(8,128)}) fusion(f32[3072]{0:T(1024)S(1)} %bitcast.156, bf16[1,768,3072]{2,1,0:T(8,128)(2,1)} %all-gather.25.cloned.1.call-done, f32[128,768]{1,0:T(8,128)S(1)} %get-tuple-element.114, f32[768]{0:T(1024)S(1)} %convert_element_type.292, f32[768]{0:T(1024)S(1)} %convert_element_type.291, ...), kind=kOutput, calls=%fused_computation.27 | convolution fusion | flops 608403456 | bytes 7490560 | tf_op jit(solution)/shard_map/dot_general | solution.py:30
  137.1 47.0 %all-gather.27.cloned.1.call-done = bf16[1,3072,768]{2,1,0:T(8,128)(2,1)} async-done(((bf16[1,384,768]{2,1,0:T(8,128)(2,1)}), bf16[1,3072,768]{2,1,0:T(8,128)(2,1)}) %all-gather.27.cloned.1.call-update) | async-done | bytes 4718608 | tf_op jit(solution)/shard_map/all_gather | solution.py:63
  184.1 5.9 %fusion.57 = (bf16[3072]{0:T(1024)(128)(2,1)}, bf16[128,3072]{1,0:T(8,128)(2,1)S(1)}) fusion(f32[128,3072]{1,0:T(8,128)} %get-tuple-element.116, bf16[128,768]{1,0:T(8,128)(2,1)S(1)} %copy-done.17, bf16[1,3072,768]{2,1,0:T(8,128)(2,1)} %all-gather.27.cloned.1.call-done), kind=kOutput, calls=%fused_computation.109 | convolution fusion | flops 613807104 | bytes 7280640 | tf_op jit(solution)/shard_map/dot_general | solution.py:40
  190.0 2.3 multiply_reduce_fusion.1
  192.3 0.2 fusion.52
  192.6 0.5 copy-done.39
  193.1 0.7 fusion.50
  193.8 0.7 copy-done.13
  194.4 1.5 convolution_convert_fusion.2
  196.2 2.1 fusion.35
  198.3 1.1 copy.49
  199.4 1.3 multiply_reduce_fusion
  201.0 0.4 fusion.39
  201.3 0.2 fusion.38
  201.6 0.4 convolution_convert_fusion.4
  202.0 3.0 convolution_convert_fusion.1
  205.1 1.0 copy-done.8
  206.1 3.7 convolution_convert_fusion
  209.8 1.1 copy-done.9
  211.0 1.0 copy.60
  211.9 4.3 %all-to-all-start = ((bf16[128,8,384]{2,0,1:T(8,128)(2,1)}), bf16[128,8,384]{2,0,1:T(8,128)(2,1)}, u32[]{:S(2)}, u32[]{:S(2)}) async-start(bf16[128,8,384]{2,0,1:T(8,128)(2,1)} %bitcast.133), calls=%async_computation.3 | async-start | bytes 1572864 | tf_op jit(solution)/shard_map/all_to_all | solution.py:251
  217.7 0.2 dynamic-update-slice.7
  217.9 1.7 convert_reduce_fusion
  219.6 0.6 convert_bitcast_fusion
  220.2 0.3 fusion.48
  220.4 0.6 fusion.53
  221.1 4.8 %multiply_reduce_fusion.2 = (bf16[768]{0:T(1024)(128)(2,1)}, f32[128]{0:T(128)}, bf16[768]{0:T(1024)(128)(2,1)}, f32[128,768]{1,0:T(8,128)}) fusion(f32[128,768]{1,0:T(8,128)S(1)} %copy-done, f32[128]{0:T(128)} %copy-done.31, f32[128]{0:T(128)S(1)} %copy-done.28, f32[768]{0:T(1024)S(1)} %convert_element_type.288, ...), kind=kOutput, calls=%fused_computation.57 | convolution fusion | flops 455539072 | bytes 4922880 | tf_op jit(solution)/shard_map/dot_general | solution.py:40
  225.9 35.2 %all-reduce.16 = (bf16[768]{0:T(1024)(128)(2,1)S(1)}, bf16[768]{0:T(1024)(128)(2,1)S(1)}, bf16[768]{0:T(1024)(128)(2,1)S(1)}, bf16[768]{0:T(1024)(128)(2,1)S(1)}...) all-reduce(bf16[768]{0:T(1024)(128)(2,1)} %copy-done.38, ...), channel_id=14, replica_groups=mesh['rep'=4,'shard'=8] {'shard'}, use_global_device_ids=true, to_apply=%add.7 | all-reduce | flops 9216 | bytes 36864
  261.2 2.8 fusion.24
  264.0 32.5 %reduce-scatter.4.cloned.1.call-done = bf16[96,2304]{1,0:T(8,128)(2,1)} async-done(((bf16[768,2304]{1,0:T(8,128)(2,1)}), bf16[96,2304]{1,0:T(8,128)(2,1)}) %reduce-scatter.4.cloned.1.call-update) | async-done | bytes 442384 | tf_op jit(solution)/shard_map/reduce_scatter | solution.py:76
  296.5 55.8 %reduce-scatter.8.cloned.1.call-done = bf16[96,3072]{1,0:T(8,128)(2,1)} async-done(((bf16[768,3072]{1,0:T(8,128)(2,1)}), bf16[96,3072]{1,0:T(8,128)(2,1)}) %reduce-scatter.8.cloned.1.call-update) | async-done | bytes 589840 | tf_op jit(solution)/shard_map/reduce_scatter | solution.py:97
  352.6 10.1 %all-reduce.18 = (bf16[1,96]{1,0:T(2,128)(2,1)S(1)}, bf16[1,96]{1,0:T(2,128)(2,1)S(1)}, bf16[1,96]{1,0:T(2,128)(2,1)S(1)}, bf16[1,96]{1,0:T(2,128)(2,1)S(1)}, bf...) all-reduce(bf16[1,96]{1,0:T(2,128)(2,1)S(1)} %dynamic-slice_bitcast, ...), channel_id=1, replica_groups=mesh['rep'=4,'shard'=8] {'rep'}, use_global_device_ids=true, to_apply=%region_13.14 | all-reduce | flops 1152 | bytes 4608 | tf_op jit(solution)/shard_map/psum | solution.py:105
  362.7 0.5 stack.79
  363.2 0.5 stack.81
  363.8 0.5 stack.85
  364.3 0.5 stack.87
  364.8 0.5 stack.91
  365.3 0.5 stack.93
  365.8 0.5 stack.95
  366.3 0.6 stack.99
  366.9 0.5 stack.103
  367.7 0.9 add_add_fusion.2
  368.6 3.9 fusion.29
  372.5 46.5 %all-reduce.22.cloned.1.call-done = (bf16[1,96,2304]{2,1,0:T(8,128)(2,1)}, bf16[1,96,768]{2,1,0:T(8,128)(2,1)}, bf16[1,96,3072]{2,1,0:T(8,128)(2,1)}, bf16[1,384,768]{2,1,0:T(8,128)(2,1)}) async-done(((bf16[1,96,2304]{2,1,0:T(8,128)(2,1)}, bf16[1,96,768]{2,1,0:T(8,128)(2,1)}, bf16[1,96,3072]{2,1,0:T(8,128)(2,1)}, bf16[1,384,768]{2,1,0:T(8,128)(2,1)}), (bf16[1,96,2304]{2,1,0:T(8,128)(2,1)}, ...) | async-done | bytes 1769488 | tf_op jit(solution)/shard_map/psum | solution.py:107
  419.0 2.1 stack.83
  421.1 1.6 stack.89
  422.7 1.1 stack.97
  423.8 1.1 stack.101
  (184 shorter events, 3.9 us)
Async XLA Ops:
  7.2 2.2 copy-start.21
  7.2 3.0 copy-start.15
  7.2 54.6 %all-gather.21.cloned.1.call-start = ((), (), s32[]{:S(2)}) async-start(), calls=%async_computation.8 | async-start | bytes 3981312 | tf_op jit(solution)/shard_map/all_gather | solution.py:54
  9.3 1.9 copy-start.16
  9.4 69.5 %all-gather.23.cloned.1.call-start = ((), (), s32[]{:S(2)}) async-start(), calls=%async_computation.9 | async-start | bytes 1327104 | tf_op jit(solution)/shard_map/all_gather | solution.py:57
  10.1 121.9 %all-gather.25.cloned.1.call-start = ((), (), s32[]{:S(2)}) async-start(), calls=%async_computation.10 | async-start | bytes 5308416 | tf_op jit(solution)/shard_map/all_gather | solution.py:61
  11.1 1.2 copy-start.4
  11.1 1.9 copy-start.47
  11.1 1.9 copy-start.48
  11.1 1.9 copy-start.49
  11.1 1.9 copy-start.50
  11.1 2.0 copy-start.51
  11.2 2.0 copy-start.52
  11.2 2.0 copy-start.53
  11.2 2.0 copy-start.42
  11.2 37.2 %copy-start = (f32[128,768]{1,0:T(8,128)S(1)}, f32[128,768]{1,0:T(8,128)}, u32[]{:S(2)}) copy-start(f32[128,768]{1,0:T(8,128)} %param.16) | copy-start | bytes 1179652
  11.2 172.9 %all-gather.27.cloned.1.call-start = ((), (), s32[]{:S(2)}) async-start(), calls=%async_computation.11 | async-start | bytes 5308416 | tf_op jit(solution)/shard_map/all_gather | solution.py:63
  12.1 36.7 %copy-start.41 = (s32[1,128]{1,0:T(1,128)S(1)}, s32[1,128]{1,0:T(1,128)}, u32[]{:S(2)}) copy-start(s32[1,128]{1,0:T(1,128)} %param.17) | copy-start | bytes 1540
  12.1 36.8 %copy-start.43 = (f32[1,384]{1,0:T(1,128)S(1)}, f32[1,384]{1,0:T(1,128)}, u32[]{:S(2)}) copy-start(f32[1,384]{1,0:T(1,128)} %param.29) | copy-start | bytes 4612
  12.2 205.7 %all-gather.19.cloned.1.call-start = ((), (), s32[]{:S(2)}) async-start(), calls=%async_computation.7 | async-start | bytes 1769472 | tf_op jit(solution)/shard_map/all_gather | solution.py:252
  12.9 251.1 %reduce-scatter.6.cloned.1.call-start = ((), (), s32[]{:S(2)}) async-start(), calls=%async_computation.5 | async-start | bytes 1327104 | tf_op jit(solution)/shard_map/reduce_scatter | solution.py:85
  48.4 13.4 %copy-start.22 = (f32[768]{0:T(1024)}, f32[768]{0:T(1024)S(1)}, u32[]{:S(2)}) copy-start(f32[768]{0:T(1024)S(1)} %convert_element_type.289) | copy-start | bytes 9220
  48.6 16.0 %copy-start.26 = (f32[128]{0:T(128)}, f32[128]{0:T(128)S(1)}, u32[]{:S(2)}) copy-start(f32[128]{0:T(128)S(1)} %broadcast_multiply_fusion.1) | copy-start | bytes 1540
  48.8 15.8 %copy-start.44 = (f32[128]{0:T(128)}, f32[128]{0:T(128)S(1)}, u32[]{:S(2)}) copy-start(f32[128]{0:T(128)S(1)} %multiply_reduce_fusion.6) | copy-start | bytes 1540
  48.8 15.8 %copy-start.31 = (f32[128]{0:T(128)}, f32[128]{0:T(128)S(1)}, u32[]{:S(2)}) copy-start(f32[128]{0:T(128)S(1)} %fusion.46) | copy-start | bytes 1540
  61.7 70.3 %copy-start.24 = (f32[768]{0:T(1024)}, f32[768]{0:T(1024)S(1)}, u32[]{:S(2)}) copy-start(f32[768]{0:T(1024)S(1)} %convert_element_type.292) | copy-start | bytes 9220
  64.9 0.8 copy-start.5
  65.7 71.4 %copy-start.11 = (bf16[12,64,128]{2,1,0:T(8,128)(2,1)}, bf16[12,64,128]{2,1,0:T(8,128)(2,1)S(1)}, u32[]{:S(2)}) copy-start(bf16[12,64,128]{2,1,0:T(8,128)(2,1)S(1)} %convolution_convert_fusion.5) | copy-start | bytes 589828
  80.6 111.7 %copy-start.29 = (f32[128]{0:T(128)}, f32[128]{0:T(128)S(1)}, u32[]{:S(2)}) copy-start(f32[128]{0:T(128)S(1)} %broadcast_multiply_fusion) | copy-start | bytes 1540
  80.8 111.5 %copy-start.34 = (f32[128]{0:T(128)}, f32[128]{0:T(128)S(1)}, u32[]{:S(2)}) copy-start(f32[128]{0:T(128)S(1)} %fusion.47) | copy-start | bytes 1540
  132.0 52.1 %copy-start.17 = (bf16[128,768]{1,0:T(8,128)(2,1)S(1)}, bf16[128,768]{1,0:T(8,128)(2,1)}, u32[]{:S(2)}) copy-start(bf16[128,768]{1,0:T(8,128)(2,1)} %convert_element_type.265) | copy-start | bytes 589828
  184.1 5.9 %copy-start.3 = (bf16[1,768,3072]{2,1,0:T(8,128)(2,1)S(1)}, bf16[1,768,3072]{2,1,0:T(8,128)(2,1)}, u32[]{:S(2)}) copy-start(bf16[1,768,3072]{2,1,0:T(8,128)(2,1)} %all-gather.25.cloned.1.call-done) | copy-start | bytes 14155780
  190.0 2.3 copy-start.7
  192.3 2.1 copy-start.12
  193.8 2.4 copy-start.2
  195.9 100.6 %reduce-scatter.4.cloned.1.call-start = ((), (), s32[]{:S(2)}) async-start(), calls=%async_computation.4 | async-start | bytes 3981312 | tf_op jit(solution)/shard_map/reduce_scatter | solution.py:76
  199.4 1.5 copy-start.6
  200.9 1.0 copy-start.23
  200.9 1.0 copy-start.27
  201.0 1.0 copy-start.32
  201.6 18.6 %copy-start.14 = (bf16[12,64,128]{2,1,0:T(8,128)(2,1)}, bf16[12,64,128]{2,1,0:T(8,128)(2,1)S(1)}, u32[]{:S(2)}) copy-start(bf16[12,64,128]{2,1,0:T(8,128)(2,1)S(1)} %fusion.38) | copy-start | bytes 589828
  205.0 1.1 copy-start.8
  205.0 1.1 copy-start.25
  205.0 1.1 copy-start.30
  205.0 1.1 copy-start.35
  205.0 147.3 %reduce-scatter.8.cloned.1.call-start = ((), (), s32[]{:S(2)}) async-start(), calls=%async_computation.6 | async-start | bytes 5308416 | tf_op jit(solution)/shard_map/reduce_scatter | solution.py:97
  209.8 1.1 copy-start.9
  210.9 6.7 %copy-start.54 = (f32[1,96]{1,0:T(1,128)S(1)}, f32[1,96]{1,0:T(1,128)}, u32[]{:S(2)}) copy-start(f32[1,96]{1,0:T(1,128)} %param.31) | copy-start | bytes 1156
  211.9 9.1 %copy-start.28 = (f32[128]{0:T(128)S(1)}, f32[128]{0:T(128)}, u32[]{:S(2)}) copy-start(f32[128]{0:T(128)} %copy-done.26) | copy-start | bytes 1540
  211.9 49.3 %all-to-all-start = ((bf16[128,8,384]{2,0,1:T(8,128)(2,1)}), bf16[128,8,384]{2,0,1:T(8,128)(2,1)}, u32[]{:S(2)}, u32[]{:S(2)}) async-start(bf16[128,8,384]{2,0,1:T(8,128)(2,1)} %bitcast.133), calls=%async_computation.3 | async-start | bytes 1572864 | tf_op jit(solution)/shard_map/all_to_all | solution.py:251
  216.3 202.7 %all-reduce.22.cloned.1.call-start = ((), (), s32[]{:S(2)}) async-start(), calls=%async_computation.12 | async-start | bytes 3538944 | tf_op jit(solution)/shard_map/psum | solution.py:107
  217.9 1.7 copy-start.38
  221.1 4.8 %copy-start.36 = (bf16[768]{0:T(1024)(128)(2,1)S(1)}, bf16[768]{0:T(1024)(128)(2,1)}, u32[]{:S(2)}) copy-start(bf16[768]{0:T(1024)(128)(2,1)} %get-tuple-element.56) | copy-start | bytes 4612
  221.1 4.8 %copy-start.37 = (bf16[768]{0:T(1024)(128)(2,1)S(1)}, bf16[768]{0:T(1024)(128)(2,1)}, u32[]{:S(2)}) copy-start(bf16[768]{0:T(1024)(128)(2,1)} %get-tuple-element.70) | copy-start | bytes 4612
  221.1 40.1 %copy-start.1 = (bf16[1024,768]{1,0:T(8,128)(2,1)S(1)}, bf16[1024,768]{1,0:T(8,128)(2,1)}, u32[]{:S(2)}) copy-start(bf16[1024,768]{1,0:T(8,128)(2,1)} %all-gather.19.cloned.1.call-done) | copy-start | bytes 4718596
  264.0 88.7 %copy-start.46 = (bf16[1,96]{1,0:T(2,128)(2,1)S(1)}, bf16[1,96]{1,0:T(2,128)(2,1)}, u32[]{:S(2)}) copy-start(bf16[1,96]{1,0:T(2,128)(2,1)} %convert_bitcast_fusion) | copy-start | bytes 580
  264.0 103.4 %copy-start.45 = (f32[128]{0:T(128)S(1)}, f32[128]{0:T(128)}, u32[]{:S(2)}) copy-start(f32[128]{0:T(128)} %copy-done.44) | copy-start | bytes 1540
  264.0 103.4 %copy-start.55 = (f32[128]{0:T(128)S(1)}, f32[128]{0:T(128)}, u32[]{:S(2)}) copy-start(f32[128]{0:T(128)} %get-tuple-element.69) | copy-start | bytes 1540
  264.0 103.5 %copy-start.20 = (f32[128,768]{1,0:T(8,128)S(1)}, f32[128,768]{1,0:T(8,128)}, u32[]{:S(2)}) copy-start(f32[128,768]{1,0:T(8,128)} %get-tuple-element.120) | copy-start | bytes 1179652
  264.0 103.5 %copy-start.33 = (f32[128]{0:T(128)S(1)}, f32[128]{0:T(128)}, u32[]{:S(2)}) copy-start(f32[128]{0:T(128)} %copy-done.31) | copy-start | bytes 1540
  264.0 103.7 %copy-start.40 = (f32[128]{0:T(128)S(1)}, f32[128]{0:T(128)}, u32[]{:S(2)}) copy-start(f32[128]{0:T(128)} %copy-done.39) | copy-start | bytes 1540
  352.3 16.3 %copy-start.10 = (bf16[128,3072]{1,0:T(8,128)(2,1)S(1)}, bf16[128,3072]{1,0:T(8,128)(2,1)}, u32[]{:S(2)}) copy-start(bf16[128,3072]{1,0:T(8,128)(2,1)} %get-tuple-element.115) | copy-start | bytes 2359300
  419.0 3.7 copy-start.19
  419.0 4.8 %copy-start.18 = (bf16[1,384,768]{2,1,0:T(8,128)(2,1)S(1)}, bf16[1,384,768]{2,1,0:T(8,128)(2,1)}, u32[]{:S(2)}) copy-start(bf16[1,384,768]{2,1,0:T(8,128)(2,1)} %get-tuple-element.100) | copy-start | bytes 1769476
  (2 other events, 1.2 us)
Sparse Core Ops, SparseCore 0:
  10.2 44.7 all-gather.20
  57.2 21.6 all-gather.22
  81.1 50.8 all-gather.24
  134.1 49.9 all-gather.26
  186.1 24.0 all-gather.18
  212.9 36.2 reduce-scatter.5
  251.5 44.9 reduce-scatter.3
  298.8 53.4 reduce-scatter.7
  356.3 62.6 all-reduce.21
where the time goes:
time: 432 us; the launch traced here: 431 us
  waiting for transfers between devices  246 us (57%)
  blocking collectives  90.6 us (21%)
  matrix products  42.4 us (10%)
  other arithmetic  20.8 us (5%)
  between operations  16.6 us (4%)
  local copies, waits for them, and re-layouts  9.89 us (2%)
  starting transfers between devices  4.9 us (1%)
    reduce_scatter x1, waiting for transfers between devices, reduce_nested_rest(): lax.psum_scatter(grads[9].astype(jnp.bfloat16), 'shard', scatter_dimensio...  55.8 us
    all_gather x1, waiting for transfers between devices, fetch_forward(): lax.all_gather(parts[9], 'shard', axis=0, tiled=True)  51.2 us
    all_gather x1, waiting for transfers between devices, fetch_forward(): lax.all_gather(parts[11], 'shard', axis=0, tiled=True)  47 us
    psum x1, waiting for transfers between devices, reduce_nested_rest(): lax.psum(owned[2].astype(jnp.bfloat16), 'rep').astype(jnp.float32)  46.5 us
    unnamed x1, blocking collectives  35.2 us
    all_gather x1, blocking collectives, fetch_forward(): lax.all_gather(parts[4], 'shard', axis=0, tiled=True)  32.5 us
    reduce_scatter x1, waiting for transfers between devices, reduce_nested_rest(): lax.psum_scatter(grads[2].astype(jnp.bfloat16), 'shard', scatter_dimensio...  32.5 us
    dot_general x4, matrix products, project_trans(): lax.dot_general(left, right, (((1,), (1,)), ((), ())), preferred_element_...  15.2 us
  transfers between devices with their start and end apart: 10, of which 6 were waited for; matrix products, arithmetic and copies ran while one was open for 14% of the time, Pallas kernels for 0%

commit v1 on v0

--- a/solution.py
+++ b/solution.py
@@ -9,6 +9,28 @@
 EPS = 1e-05
 GELU_C = 0.7978845608028654
 NEG_FILL = -1e30
+
+
+def joined_along(parts, dim):
+    lengths = list(parts.shape[1:])
+    lengths[dim] *= parts.shape[0]
+    return jnp.moveaxis(parts, 0, dim).reshape(lengths)
+
+
+def gather_around(value, axis, dim):
+    devices = lax.axis_size(axis)
+    pairs = [(i, (i + 1) % devices) for i in range(devices)]
+    back = [(b, a) for a, b in pairs]
+    lower, upper = ([], [])
+    for lap in range(devices - 1):
+        if lap % 2 == 0:
+            lower.append(lax.ppermute(lower[-1] if lower else value, axis, pairs))
+        else:
+            upper.append(lax.ppermute(upper[-1] if upper else value, axis, back))
+    blocks = jnp.stack([*lower[::-1], value, *upper])
+    shift = lax.axis_index(axis) - len(lower)
+    blocks = blocks[(jnp.arange(devices) - shift) % devices]
+    return joined_along(blocks, dim)
 
 
 def norm(values_in, gains, shifts):
@@ -60,7 +82,7 @@
         lax.all_gather(parts[8], "shard", axis=0, tiled=True),
         lax.all_gather(parts[9], "shard", axis=0, tiled=True),
         lax.all_gather(parts[10], "shard", axis=0, tiled=True),
-        lax.all_gather(parts[11], "shard", axis=0, tiled=True),
+        gather_around(parts[11], "shard", 0),
         lax.all_gather(parts[12], "shard", axis=0, tiled=True),
     )
 

time: 432 us -> 404 us (0.935)
  waiting for transfers between devices: 246 us -> 177 us
  local copies, waits for them, and re-layouts: 9.89 us -> 26.8 us
  blocking collectives: 90.6 us -> 106 us
  starting transfers between devices: 4.9 us -> 17.8 us
    all_gather x1 -> x0, waiting for transfers between devices: 47 us -> none  [fetch_forward(): lax.all_gather(parts[11], 'shard', axis=0, tiled=True)]
    ppermute x0 -> x7, waiting for transfers between devices: none -> 44.9 us  [the longest x4 34 us: gather_around(): lower.append(lax.ppermute(lower[-1] if lower else value, axis, pairs))]
    all_gather x1, waiting for transfers between devices: 51.2 us -> 6.93 us  [fetch_forward(): lax.all_gather(parts[9], 'shard', axis=0, tiled=True)]
    all_gather x1, waiting for transfers between devices: 13.2 us -> 0.01 us  [fetch_forward(): lax.all_gather(parts[5], 'shard', axis=0, tiled=True)]
    unnamed x131 -> x143, local copies, waits for them, and re-layouts: 6.02 us -> 14.9 us
    ppermute x0 -> x7, starting transfers between devices: none -> 8.71 us  [the longest x3 7.03 us: gather_around(): upper.append(lax.ppermute(upper[-1] if upper else value, axis, back))]
    all_gather x1, blocking collectives: 12.8 us -> 20.4 us  [fetch_forward(): lax.all_gather(parts[10], 'shard', axis=0, tiled=True)]
    reduce_scatter x1, waiting for transfers between devices: 32.5 us -> 26 us  [reduce_nested_rest(): lax.psum_scatter(grads[2].astype(jnp.bfloat16), 'shard', scatter_dimensio...]
  transfers between devices with their start and end apart: 10 -> 16, of which waited for: 6 -> 7; matrix products, arithmetic and copies ran while one was open for 14% -> 19% of each run, Pallas kernels for 0% -> 0%
where the time goes in v1:
time: 404 us; the launch traced here: 403 us
  waiting for transfers between devices  177 us (44%)
  blocking collectives  106 us (26%)
  matrix products  39.1 us (10%)
  local copies, waits for them, and re-layouts  26.8 us (7%)
  other arithmetic  20 us (5%)
  starting transfers between devices  17.8 us (4%)
  between operations  16.9 us (4%)
    reduce_scatter x1, waiting for transfers between devices, reduce_nested_rest(): lax.psum_scatter(grads[9].astype(jnp.bfloat16), 'shard', scatter_dimensio...  55.7 us
    psum x1, waiting for transfers between devices, reduce_nested_rest(): lax.psum(owned[2].astype(jnp.bfloat16), 'rep').astype(jnp.float32)  43.2 us
    all_gather x1, blocking collectives, fetch_forward(): lax.all_gather(parts[4], 'shard', axis=0, tiled=True)  38.1 us
    unnamed x1, blocking collectives  36.7 us
    ppermute x4, waiting for transfers between devices, gather_around(): lower.append(lax.ppermute(lower[-1] if lower else value, axis, pairs))  34 us
    reduce_scatter x1, waiting for transfers between devices, reduce_nested_rest(): lax.psum_scatter(grads[2].astype(jnp.bfloat16), 'shard', scatter_dimensio...  26 us
    all_gather x1, blocking collectives, fetch_forward(): lax.all_gather(parts[10], 'shard', axis=0, tiled=True)  20.4 us
    unnamed x143, local copies, waits for them, and re-layouts  14.9 us
  transfers between devices with their start and end apart: 16, of which 7 were waited for; matrix products, arithmetic and copies ran while one was open for 19% of the time, Pallas kernels for 0%

profile of v1, /device:TPU:0, one launch (start us, length us, event | category | flops | bytes accessed | tf_op | source)
XLA Modules:
  0.0 403.3 jit_solution(17041717350738038368)
XLA Ops:
  7.2 2.1 convert_element_type.232
  9.4 0.7 convert_element_type.243
  10.2 0.9 convert_element_type.255
  11.3 0.5 collective-permute-start
  11.9 4.1 %collective-permute-start.4 = (bf16[384,768]{1,0:T(8,128)(2,1)S(1)}, bf16[384,768]{1,0:T(8,128)(2,1)S(1)}, u32[]{:S(2)}, u32[]{:S(2)}) collective-permute-start(bf16[384,768]{1,0:T(8,128)(2,1)S(1)} %convert_bitcast_fusion), channel_id=1, source_target_pairs={{1,0},{2,1},{3,2},{4,3},{5,4},{6,5},{7,6},{0,7},{9,8},{10,9},{11,1... | collective-permute-start | bytes 1769480 | tf_op jit(solution)/shard_map/ppermute | solution.py:29
  16.0 0.7 convert_element_type.266
  16.8 0.6 fusion.45
  18.8 10.5 %collective-permute-done = bf16[384,768]{1,0:T(8,128)(2,1)} collective-permute-done((bf16[384,768]{1,0:T(8,128)(2,1)S(1)}, bf16[384,768]{1,0:T(8,128)(2,1)}, u32[]{:S(2)}, u32[]{:S(2)}) %collective-permute-start) | collective-permute-done | bytes 589856 | tf_op jit(solution)/shard_map/ppermute | solution.py:27
  29.2 0.6 collective-permute-start.1
  30.6 23.6 %collective-permute-done.1 = bf16[384,768]{1,0:T(8,128)(2,1)} collective-permute-done((bf16[384,768]{1,0:T(8,128)(2,1)}, bf16[384,768]{1,0:T(8,128)(2,1)}, u32[]{:S(2)}, u32[]{:S(2)}) %collective-permute-start.1) | collective-permute-done | bytes 589856 | tf_op jit(solution)/shard_map/ppermute | solution.py:27
  54.5 38.1 %all-reduce.17 = (bf16[768]{0:T(1024)(128)(2,1)S(1)}, bf16[768]{0:T(1024)(128)(2,1)S(1)}, bf16[768]{0:T(1024)(128)(2,1)S(1)}, bf16[768]{0:T(1024)(128)(2,1)S(1)}...) all-reduce(bf16[768]{0:T(1024)(128)(2,1)S(1)} %dynamic-update-slice, ...), channel_id=6, replica_groups=mesh['rep'=4,'shard'=8] {'shard'}, use_global_device_ids=true, to_apply=%add.3 | all-reduce | flops 5376 | bytes 21504 | tf_op jit(solution)/shard_map/all_gather | solution.py:78
  93.4 20.4 %all-gather.10 = bf16[1,3072]{1,0:T(2,128)(2,1)S(1)} all-gather(bf16[1,384]{1,0:T(2,128)(2,1)S(1)} %convert_element_type.257), channel_id=12, replica_groups=mesh['rep'=4,'shard'=8] {'shard'}, dimensions={1}, use_global_device_ids=true | all-gather | bytes 6912 | tf_op jit(solution)/shard_map/all_gather | solution.py:84
  114.1 2.9 collective-permute-start.6
  117.0 0.8 bitcast_dynamic-update-slice_fusion.6
  117.9 1.9 bitcast_dynamic-update-slice_fusion.5
  119.8 1.9 bitcast_dynamic-update-slice_fusion.4
  121.7 1.9 bitcast_dynamic-update-slice_fusion.3
  123.7 0.9 convert_dynamic-update-slice_fusion
  124.5 0.9 bitcast_dynamic-update-slice_fusion.2
  125.5 0.8 bitcast_dynamic-update-slice_fusion.1
  126.3 10.9 %collective-permute-done.6 = bf16[384,768]{1,0:T(8,128)(2,1)S(1)} collective-permute-done((bf16[384,768]{1,0:T(8,128)(2,1)S(1)}, bf16[384,768]{1,0:T(8,128)(2,1)S(1)}, u32[]{:S(2)}, u32[]{:S(2)}) %collective-permute-start.6) | collective-permute-done | bytes 589856 | tf_op jit(solution)/shard_map/ppermute | solution.py:29
  137.2 0.8 bitcast_dynamic-update-slice_fusion
  138.0 5.3 %gather_fusion = bf16[8,384,768]{2,1,0:T(8,128)(2,1)} fusion(bf16[8,384,768]{2,1,0:T(8,128)(2,1)} %bitcast_dynamic-update-slice_fusion, s32[1024]{0:T(1024)S(1)} %pad_clamp_fusion), kind=kCustom, calls=%fused_computation | custom fusion | bytes 9437216 | tf_op jit(solution)/shard_map/gather | solution.py:32
  143.4 2.7 fusion.7
  147.2 1.7 fusion.47
  149.1 6.9 %all-gather.23.cloned.1.call-done = bf16[1,768,3072]{2,1,0:T(8,128)(2,1)} async-done(((bf16[1,96,3072]{2,1,0:T(8,128)(2,1)}), bf16[1,768,3072]{2,1,0:T(8,128)(2,1)}) %all-gather.23.cloned.1.call-update) | async-done | bytes 4718608 | tf_op jit(solution)/shard_map/all_gather | solution.py:83
  156.1 4.7 %multiply_convert_fusion = (bf16[128,3072]{1,0:T(8,128)(2,1)}, f32[128,3072]{1,0:T(8,128)S(1)}) fusion(f32[3072]{0:T(1024)S(1)} %bitcast.173, bf16[1,768,3072]{2,1,0:T(8,128)(2,1)} %all-gather.23.cloned.1.call-done, f32[128,768]{1,0:T(8,128)S(1)} %get-tuple-element.114, f32[768]{0:T(1024)S(1)} %convert_element_type.293, f32[768]{0:T(1024)S(1)} %convert_element_type.292, ...), kind=kOutput, calls=%fused_computation.25 | convolution fusion | flops 608403456 | bytes 7490560 | tf_op jit(solution)/shard_map/dot_general | solution.py:52
  160.8 5.4 %fusion.48 = (bf16[3072]{0:T(1024)(128)(2,1)}, bf16[128,3072]{1,0:T(8,128)(2,1)S(1)}) fusion(f32[128,3072]{1,0:T(8,128)S(1)} %get-tuple-element.116, bf16[3072,768]{1,0:T(8,128)(2,1)} %bitcast.146, bf16[128,768]{1,0:T(8,128)(2,1)S(1)} %copy-done.17), kind=kOutput, calls=%fused_computation.123 | convolution fusion | flops 613807104 | bytes 7280640 | tf_op jit(solution)/shard_map/dot_general | solution.py:62
  166.2 2.3 multiply_reduce_fusion.1
  168.8 0.7 copy-done.5
  169.5 0.7 fusion.41
  170.2 1.5 convolution_convert_fusion.2
  172.0 0.5 fusion.24
  172.7 1.3 multiply_reduce_fusion
  175.3 3.1 convolution_convert_fusion.1
  178.5 1.1 copy-done.10
  179.5 3.7 convolution_convert_fusion
  183.3 1.1 copy-done.11
  184.4 1.0 copy.60
  185.4 8.6 %all-to-all-start = ((bf16[128,8,384]{2,0,1:T(8,128)(2,1)}), bf16[128,8,384]{2,0,1:T(8,128)(2,1)S(1)}, u32[]{:S(2)}, u32[]{:S(2)}) async-start(bf16[128,8,384]{2,0,1:T(8,128)(2,1)} %bitcast.145), calls=%async_computation.3 | async-start | bytes 1572864 | tf_op jit(solution)/shard_map/all_to_all | solution.py:273
  195.6 1.7 convert_reduce_fusion
  197.3 0.6 convert_bitcast_fusion.1
  198.1 0.6 fusion.44
  198.8 5.1 %multiply_reduce_fusion.2 = (bf16[768]{0:T(1024)(128)(2,1)}, f32[128]{0:T(128)}, bf16[768]{0:T(1024)(128)(2,1)}, f32[128,768]{1,0:T(8,128)}) fusion(f32[128,768]{1,0:T(8,128)S(1)} %copy-done, f32[128]{0:T(128)S(1)} %copy-done.34, f32[128]{0:T(128)S(1)} %copy-done.29, f32[768]{0:T(1024)S(1)} %convert_element_type.289, ...), kind=kOutput, calls=%fused_computation.62 | convolution fusion | flops 455539072 | bytes 4922880 | tf_op jit(solution)/shard_map/dot_general | solution.py:62
  203.8 36.7 %all-reduce.16 = (bf16[768]{0:T(1024)(128)(2,1)}, bf16[768]{0:T(1024)(128)(2,1)}, bf16[768]{0:T(1024)(128)(2,1)}, bf16[768]{0:T(1024)(128)(2,1)}, bf16[768]{0:T(...) all-reduce(bf16[768]{0:T(1024)(128)(2,1)} %copy-done.38, ...), channel_id=13, replica_groups=mesh['rep'=4,'shard'=8] {'shard'}, use_global_device_ids=true, to_apply=%add.7 | all-reduce | flops 9216 | bytes 36864
  240.5 0.8 dynamic-slice.24
  241.3 1.6 fusion.18
  243.0 26.0 %reduce-scatter.4.cloned.1.call-done = bf16[96,2304]{1,0:T(8,128)(2,1)} async-done(((bf16[768,2304]{1,0:T(8,128)(2,1)}), bf16[96,2304]{1,0:T(8,128)(2,1)}) %reduce-scatter.4.cloned.1.call-update) | async-done | bytes 442384 | tf_op jit(solution)/shard_map/reduce_scatter | solution.py:98
  269.0 55.7 %reduce-scatter.8.cloned.1.call-done = bf16[96,3072]{1,0:T(8,128)(2,1)} async-done(((bf16[768,3072]{1,0:T(8,128)(2,1)}), bf16[96,3072]{1,0:T(8,128)(2,1)}) %reduce-scatter.8.cloned.1.call-update) | async-done | bytes 589840 | tf_op jit(solution)/shard_map/reduce_scatter | solution.py:119
  324.8 0.8 dynamic-slice_bitcast_fusion.6
  325.6 0.8 dynamic-slice_bitcast_fusion
  326.4 0.8 dynamic-slice_bitcast_fusion.2
  327.1 0.8 dynamic-slice_bitcast_fusion.4
  327.9 10.5 %all-reduce.18 = (bf16[1,96]{1,0:T(2,128)(2,1)S(1)}, bf16[1,96]{1,0:T(2,128)(2,1)S(1)}, bf16[1,96]{1,0:T(2,128)(2,1)S(1)}, bf16[1,96]{1,0:T(2,128)(2,1)S(1)}, bf...) all-reduce(bf16[1,96]{1,0:T(2,128)(2,1)S(1)} %dynamic-slice_bitcast, ...), channel_id=1, replica_groups=mesh['rep'=4,'shard'=8] {'rep'}, use_global_device_ids=true, to_apply=%region_13.14 | all-reduce | flops 1152 | bytes 4608 | tf_op jit(solution)/shard_map/psum | solution.py:127
  338.4 0.6 stack.132
  338.9 0.5 stack.112
  341.5 0.5 stack.126
  343.3 0.9 add_add_fusion.2
  344.2 4.0 fusion.20
  348.2 43.2 %all-reduce.22.cloned.1.call-done = (bf16[1,96,2304]{2,1,0:T(8,128)(2,1)}, bf16[1,96,768]{2,1,0:T(8,128)(2,1)}, bf16[1,96,3072]{2,1,0:T(8,128)(2,1)}, bf16[1,384,768]{2,1,0:T(8,128)(2,1)}) async-done(((bf16[1,96,2304]{2,1,0:T(8,128)(2,1)}, bf16[1,96,768]{2,1,0:T(8,128)(2,1)}, bf16[1,96,3072]{2,1,0:T(8,128)(2,1)}, bf16[1,384,768]{2,1,0:T(8,128)(2,1)}), (bf16[1,96,2304]{2,1,0:T(8,128)(2,1)}, ...) | async-done | bytes 1769488 | tf_op jit(solution)/shard_map/psum | solution.py:129
  391.4 2.3 stack.130
  393.7 1.1 stack.134
  394.8 1.0 stack.116
  395.8 0.7 stack.122
  (213 shorter events, 10.3 us)
Async XLA Ops:
  7.2 2.2 copy-start.21
  7.2 3.0 copy-start.16
  7.2 136.2 %all-gather.19.cloned.1.call-start = ((), (), s32[]{:S(2)}) async-start(), calls=%async_computation.8 | async-start | bytes 3981312 | tf_op jit(solution)/shard_map/all_gather | solution.py:76
  9.3 1.9 copy-start.2
  9.4 137.8 %all-gather.21.cloned.1.call-start = ((), (), s32[]{:S(2)}) async-start(), calls=%async_computation.9 | async-start | bytes 1327104 | tf_op jit(solution)/shard_map/all_gather | solution.py:79
  10.1 146.0 %all-gather.23.cloned.1.call-start = ((), (), s32[]{:S(2)}) async-start(), calls=%async_computation.10 | async-start | bytes 5308416 | tf_op jit(solution)/shard_map/all_gather | solution.py:83
  11.1 4.9 %copy-start.4 = (f32[128,768]{1,0:T(8,128)S(1)}, f32[128,768]{1,0:T(8,128)}, u32[]{:S(2)}) copy-start(f32[128,768]{1,0:T(8,128)} %param.18) | copy-start | bytes 1179652
  11.1 5.7 %copy-start.43 = (u32[32]{0:T(128)S(1)}, u32[32]{0:T(128)}, u32[]{:S(2)}) copy-start(u32[32]{0:T(128)} %constant.108) | copy-start | bytes 388
  11.1 6.9 %copy-start.48 = (f32[1,96]{1,0:T(1,128)S(1)}, f32[1,96]{1,0:T(1,128)}, u32[]{:S(2)}) copy-start(f32[1,96]{1,0:T(1,128)} %param.19) | copy-start | bytes 1156
  11.1 7.2 %copy-start.49 = (f32[1,96]{1,0:T(1,128)S(1)}, f32[1,96]{1,0:T(1,128)}, u32[]{:S(2)}) copy-start(f32[1,96]{1,0:T(1,128)} %param.20) | copy-start | bytes 1156
  11.1 7.4 %copy-start.50 = (f32[1,96]{1,0:T(1,128)S(1)}, f32[1,96]{1,0:T(1,128)}, u32[]{:S(2)}) copy-start(f32[1,96]{1,0:T(1,128)} %param.22) | copy-start | bytes 1156
  11.1 18.8 %copy-start.51 = (f32[1,96]{1,0:T(1,128)S(1)}, f32[1,96]{1,0:T(1,128)}, u32[]{:S(2)}) copy-start(f32[1,96]{1,0:T(1,128)} %param.23) | copy-start | bytes 1156
  11.1 19.0 %copy-start.52 = (f32[1,96]{1,0:T(1,128)S(1)}, f32[1,96]{1,0:T(1,128)}, u32[]{:S(2)}) copy-start(f32[1,96]{1,0:T(1,128)} %param.25) | copy-start | bytes 1156
  11.1 19.2 %copy-start.53 = (f32[1,96]{1,0:T(1,128)S(1)}, f32[1,96]{1,0:T(1,128)}, u32[]{:S(2)}) copy-start(f32[1,96]{1,0:T(1,128)} %param.26) | copy-start | bytes 1156
  11.1 43.0 %copy-start.54 = (f32[1,96]{1,0:T(1,128)S(1)}, f32[1,96]{1,0:T(1,128)}, u32[]{:S(2)}) copy-start(f32[1,96]{1,0:T(1,128)} %param.27) | copy-start | bytes 1156
  11.1 43.3 %copy-start = (f32[128,768]{1,0:T(8,128)S(1)}, f32[128,768]{1,0:T(8,128)}, u32[]{:S(2)}) copy-start(f32[128,768]{1,0:T(8,128)} %param.16) | copy-start | bytes 1179652
  11.2 82.2 %copy-start.44 = (f32[1,384]{1,0:T(1,128)S(1)}, f32[1,384]{1,0:T(1,128)}, u32[]{:S(2)}) copy-start(f32[1,384]{1,0:T(1,128)} %param.29) | copy-start | bytes 4612
  11.2 102.8 %copy-start.42 = (s32[1,128]{1,0:T(1,128)S(1)}, s32[1,128]{1,0:T(1,128)}, u32[]{:S(2)}) copy-start(s32[1,128]{1,0:T(1,128)} %param.17) | copy-start | bytes 1540
  11.2 184.4 %all-gather.17.cloned.1.call-start = ((), (), s32[]{:S(2)}) async-start(), calls=%async_computation.7 | async-start | bytes 1769472 | tf_op jit(solution)/shard_map/all_gather | solution.py:274
  11.3 17.9 %collective-permute-start = (bf16[384,768]{1,0:T(8,128)(2,1)S(1)}, bf16[384,768]{1,0:T(8,128)(2,1)}, u32[]{:S(2)}, u32[]{:S(2)}) collective-permute-start(bf16[384,768]{1,0:T(8,128)(2,1)S(1)} %convert_bitcast_fusion), channel_id=1, source_target_pairs={{0,1},{1,2},{2,3},{3,4},{4,5},{5,6},{6,7},{7,0},{8,9},{9,10},{10,1... | collective-permute-start | bytes 1769480 | tf_op jit(solution)/shard_map/ppermute | solution.py:27
  11.9 80.8 %collective-permute-start.4 = (bf16[384,768]{1,0:T(8,128)(2,1)S(1)}, bf16[384,768]{1,0:T(8,128)(2,1)S(1)}, u32[]{:S(2)}, u32[]{:S(2)}) collective-permute-start(bf16[384,768]{1,0:T(8,128)(2,1)S(1)} %convert_bitcast_fusion), channel_id=1, source_target_pairs={{1,0},{2,1},{3,2},{4,3},{5,4},{6,5},{7,6},{0,7},{9,8},{10,9},{11,1... | collective-permute-start | bytes 1769480 | tf_op jit(solution)/shard_map/ppermute | solution.py:29
  16.7 226.3 %reduce-scatter.6.cloned.1.call-start = ((), (), s32[]{:S(2)}) async-start(), calls=%async_computation.5 | async-start | bytes 1327104 | tf_op jit(solution)/shard_map/reduce_scatter | solution.py:107
  29.2 24.9 %collective-permute-start.1 = (bf16[384,768]{1,0:T(8,128)(2,1)}, bf16[384,768]{1,0:T(8,128)(2,1)}, u32[]{:S(2)}, u32[]{:S(2)}) collective-permute-start(bf16[384,768]{1,0:T(8,128)(2,1)} %collective-permute-done), channel_id=1, source_target_pairs={{0,1},{1,2},{2,3},{3,4},{4,5},{5,6},{6,7},{7,0},{8,9},{9,10},{10,1... | collective-permute-start | bytes 1769480 | tf_op jit(solution)/shard_map/ppermute | solution.py:27
  54.2 38.6 %collective-permute-start.2 = (bf16[384,768]{1,0:T(8,128)(2,1)}, bf16[384,768]{1,0:T(8,128)(2,1)}, u32[]{:S(2)}, u32[]{:S(2)}) collective-permute-start(bf16[384,768]{1,0:T(8,128)(2,1)} %collective-permute-done.1), channel_id=1, source_target_pairs={{0,1},{1,2},{2,3},{3,4},{4,5},{5,6},{6,7},{7,0},{8,9},{9,10},{10,1... | collective-permute-start | bytes 1769480 | tf_op jit(solution)/shard_map/ppermute | solution.py:27
  92.7 50.7 %copy-start.27 = (f32[128]{0:T(128)}, f32[128]{0:T(128)S(1)}, u32[]{:S(2)}) copy-start(f32[128]{0:T(128)S(1)} %broadcast_multiply_fusion.1) | copy-start | bytes 1540
  92.7 21.4 %collective-permute-start.5 = (bf16[384,768]{1,0:T(8,128)(2,1)S(1)}, bf16[384,768]{1,0:T(8,128)(2,1)S(1)}, u32[]{:S(2)}, u32[]{:S(2)}) collective-permute-start(bf16[384,768]{1,0:T(8,128)(2,1)S(1)} %collective-permute-done.4), channel_id=1, source_target_pairs={{1,0},{2,1},{3,2},{4,3},{5,4},{6,5},{7,6},{0,7},{9,8},{10,9},{11,1... | collective-permute-start | bytes 1769480 | tf_op jit(solution)/shard_map/ppermute | solution.py:29
  92.8 24.3 %collective-permute-start.3 = (bf16[384,768]{1,0:T(8,128)(2,1)}, bf16[384,768]{1,0:T(8,128)(2,1)S(1)}, u32[]{:S(2)}, u32[]{:S(2)}) collective-permute-start(bf16[384,768]{1,0:T(8,128)(2,1)} %collective-permute-done.2), channel_id=1, source_target_pairs={{0,1},{1,2},{2,3},{3,4},{4,5},{5,6},{6,7},{7,0},{8,9},{9,10},{10,1... | collective-permute-start | bytes 1769480 | tf_op jit(solution)/shard_map/ppermute | solution.py:27
  93.3 50.1 %copy-start.23 = (f32[768]{0:T(1024)}, f32[768]{0:T(1024)S(1)}, u32[]{:S(2)}) copy-start(f32[768]{0:T(1024)S(1)} %convert_element_type.290) | copy-start | bytes 9220
  93.3 62.7 %copy-start.25 = (f32[768]{0:T(1024)}, f32[768]{0:T(1024)S(1)}, u32[]{:S(2)}) copy-start(f32[768]{0:T(1024)S(1)} %convert_element_type.293) | copy-start | bytes 9220
  114.0 7.7 %copy-start.45 = (f32[128]{0:T(128)}, f32[128]{0:T(128)S(1)}, u32[]{:S(2)}) copy-start(f32[128]{0:T(128)S(1)} %multiply_reduce_fusion.6) | copy-start | bytes 1540
  114.0 29.4 %copy-start.32 = (f32[128]{0:T(128)}, f32[128]{0:T(128)S(1)}, u32[]{:S(2)}) copy-start(f32[128]{0:T(128)S(1)} %fusion.37) | copy-start | bytes 1540
  114.1 23.0 %collective-permute-start.6 = (bf16[384,768]{1,0:T(8,128)(2,1)S(1)}, bf16[384,768]{1,0:T(8,128)(2,1)S(1)}, u32[]{:S(2)}, u32[]{:S(2)}) collective-permute-start(bf16[384,768]{1,0:T(8,128)(2,1)S(1)} %collective-permute-done.5), channel_id=1, source_target_pairs={{1,0},{2,1},{3,2},{4,3},{5,4},{6,5},{7,6},{0,7},{9,8},{10,9},{11,1... | collective-permute-start | bytes 1769480 | tf_op jit(solution)/shard_map/ppermute | solution.py:29
  148.9 19.6 %copy-start.30 = (f32[128]{0:T(128)}, f32[128]{0:T(128)S(1)}, u32[]{:S(2)}) copy-start(f32[128]{0:T(128)S(1)} %broadcast_multiply_fusion) | copy-start | bytes 1540
  149.1 19.4 %copy-start.35 = (f32[128]{0:T(128)}, f32[128]{0:T(128)S(1)}, u32[]{:S(2)}) copy-start(f32[128]{0:T(128)S(1)} %fusion.38) | copy-start | bytes 1540
  156.1 4.7 %copy-start.17 = (bf16[128,768]{1,0:T(8,128)(2,1)S(1)}, bf16[128,768]{1,0:T(8,128)(2,1)}, u32[]{:S(2)}) copy-start(bf16[128,768]{1,0:T(8,128)(2,1)} %convert_element_type.266) | copy-start | bytes 589828
  156.1 10.1 %slice-start = ((s8[4718592]{0:T(1024)(128)(4,1)}), s8[4194304]{0:T(1024)(128)(4,1)S(1)}, s32[]{:S(2)}) async-start(s8[4718592]{0:T(1024)(128)(4,1)} %bitcast.148), calls=%async_computation.12 | async-start | bytes 8388608
  160.8 5.4 %slice-start.1 = ((s8[4718592]{0:T(1024)(128)(4,1)}), s8[524288]{0:T(1024)(128)(4,1)S(1)}, s32[]{:S(2)}) async-start(s8[4718592]{0:T(1024)(128)(4,1)} %bitcast.148), calls=%async_computation.13 | async-start | bytes 1048576
  166.2 2.3 copy-start.9
  170.2 1.7 copy-start.3
  171.7 97.3 %reduce-scatter.4.cloned.1.call-start = ((), (), s32[]{:S(2)}) async-start(), calls=%async_computation.4 | async-start | bytes 3981312 | tf_op jit(solution)/shard_map/reduce_scatter | solution.py:98
  172.7 1.5 copy-start.8
  174.5 23.4 %copy-start.14 = (bf16[12,64,128]{2,1,0:T(8,128)(2,1)}, bf16[12,64,128]{2,1,0:T(8,128)(2,1)S(1)}, u32[]{:S(2)}) copy-start(bf16[12,64,128]{2,1,0:T(8,128)(2,1)S(1)} %fusion.27) | copy-start | bytes 589828
  174.9 23.0 %copy-start.15 = (bf16[12,64,128]{2,1,0:T(8,128)(2,1)}, bf16[12,64,128]{2,1,0:T(8,128)(2,1)S(1)}, u32[]{:S(2)}) copy-start(bf16[12,64,128]{2,1,0:T(8,128)(2,1)S(1)} %fusion.28) | copy-start | bytes 589828
  175.2 22.6 %copy-start.13 = (bf16[12,64,128]{2,1,0:T(8,128)(2,1)}, bf16[12,64,128]{2,1,0:T(8,128)(2,1)S(1)}, u32[]{:S(2)}) copy-start(bf16[12,64,128]{2,1,0:T(8,128)(2,1)S(1)} %convolution_convert_fusion.4) | copy-start | bytes 589828
  178.4 146.3 %reduce-scatter.8.cloned.1.call-start = ((), (), s32[]{:S(2)}) async-start(), calls=%async_computation.6 | async-start | bytes 5308416 | tf_op jit(solution)/shard_map/reduce_scatter | solution.py:119
  184.4 10.9 %copy-start.55 = (f32[1,96]{1,0:T(1,128)S(1)}, f32[1,96]{1,0:T(1,128)}, u32[]{:S(2)}) copy-start(f32[1,96]{1,0:T(1,128)} %param.31) | copy-start | bytes 1156
  185.3 13.4 %copy-start.29 = (f32[128]{0:T(128)S(1)}, f32[128]{0:T(128)}, u32[]{:S(2)}) copy-start(f32[128]{0:T(128)} %copy-done.27) | copy-start | bytes 1540
  185.3 13.4 %copy-start.34 = (f32[128]{0:T(128)S(1)}, f32[128]{0:T(128)}, u32[]{:S(2)}) copy-start(f32[128]{0:T(128)} %copy-done.32) | copy-start | bytes 1540
  185.4 55.9 %all-to-all-start = ((bf16[128,8,384]{2,0,1:T(8,128)(2,1)}), bf16[128,8,384]{2,0,1:T(8,128)(2,1)S(1)}, u32[]{:S(2)}, u32[]{:S(2)}) async-start(bf16[128,8,384]{2,0,1:T(8,128)(2,1)} %bitcast.145), calls=%async_computation.3 | async-start | bytes 1572864 | tf_op jit(solution)/shard_map/all_to_all | solution.py:273
  194.0 197.5 %all-reduce.22.cloned.1.call-start = ((), (), s32[]{:S(2)}) async-start(), calls=%async_computation.11 | async-start | bytes 3538944 | tf_op jit(solution)/shard_map/psum | solution.py:129
  195.6 1.7 copy-start.38
  198.7 5.1 %copy-start.37 = (bf16[768]{0:T(1024)(128)(2,1)S(1)}, bf16[768]{0:T(1024)(128)(2,1)}, u32[]{:S(2)}) copy-start(bf16[768]{0:T(1024)(128)(2,1)} %get-tuple-element.56) | copy-start | bytes 4612
  198.7 42.5 %copy-start.1 = (bf16[1024,768]{1,0:T(8,128)(2,1)S(1)}, bf16[1024,768]{1,0:T(8,128)(2,1)}, u32[]{:S(2)}) copy-start(bf16[1024,768]{1,0:T(8,128)(2,1)} %all-gather.17.cloned.1.call-done) | copy-start | bytes 4718596
  242.9 85.0 %copy-start.47 = (bf16[1,96]{1,0:T(2,128)(2,1)S(1)}, bf16[1,96]{1,0:T(2,128)(2,1)}, u32[]{:S(2)}) copy-start(bf16[1,96]{1,0:T(2,128)(2,1)} %convert_bitcast_fusion.1) | copy-start | bytes 580
  242.9 100.1 %copy-start.41 = (bf16[768]{0:T(1024)(128)(2,1)S(1)}, bf16[768]{0:T(1024)(128)(2,1)}, u32[]{:S(2)}) copy-start(bf16[768]{0:T(1024)(128)(2,1)} %get-tuple-element.72) | copy-start | bytes 4612
  242.9 100.1 %copy-start.46 = (f32[128]{0:T(128)S(1)}, f32[128]{0:T(128)}, u32[]{:S(2)}) copy-start(f32[128]{0:T(128)} %copy-done.45) | copy-start | bytes 1540
  242.9 100.1 %copy-start.56 = (f32[128]{0:T(128)S(1)}, f32[128]{0:T(128)}, u32[]{:S(2)}) copy-start(f32[128]{0:T(128)} %get-tuple-element.69) | copy-start | bytes 1540
  242.9 100.2 %copy-start.20 = (f32[128,768]{1,0:T(8,128)S(1)}, f32[128,768]{1,0:T(8,128)}, u32[]{:S(2)}) copy-start(f32[128,768]{1,0:T(8,128)} %get-tuple-element.120) | copy-start | bytes 1179652
  242.9 100.4 %copy-start.6 = (f32[128,768]{1,0:T(8,128)S(1)}, f32[128,768]{1,0:T(8,128)}, u32[]{:S(2)}) copy-start(f32[128,768]{1,0:T(8,128)} %copy-done.5) | copy-start | bytes 1179652
  242.9 100.4 %copy-start.40 = (f32[128]{0:T(128)S(1)}, f32[128]{0:T(128)}, u32[]{:S(2)}) copy-start(f32[128]{0:T(128)} %copy-done.39) | copy-start | bytes 1540
  324.8 19.4 %copy-start.12 = (bf16[128,3072]{1,0:T(8,128)(2,1)S(1)}, bf16[128,3072]{1,0:T(8,128)(2,1)}, u32[]{:S(2)}) copy-start(bf16[128,3072]{1,0:T(8,128)(2,1)} %get-tuple-element.115) | copy-start | bytes 2359300
  391.4 2.3 copy-start.18
  391.4 3.4 copy-start.19
  393.7 2.1 copy-start.22
  (11 other events, 12.0 us)
Sparse Core Ops, SparseCore 0:
  10.2 58.5 all-gather.18
  71.1 25.9 all-gather.20
  99.3 56.7 all-gather.22
  158.1 24.0 all-gather.16
  184.9 35.5 reduce-scatter.5
  222.7 46.2 reduce-scatter.3
  271.3 53.3 reduce-scatter.7
  328.8 62.6 all-reduce.21
